TPU v7x, 32 devices: a whole 2x2x4 slice. The times are simulated.
32 devices in a mesh: base: 16 (over z, x, core), band: 2 (over y).
Axes of the slice: x: 2, y: 2, z: 4, core: 2. Of those that a mesh axis runs over, the one named last changes fastest.
Arguments:
- coherency: float32 [16, 16, 8, 4096], P('band', None, None, 'base'), may hold values from -1.5 to 1.5
- observed: float32 [16, 8, 4096], P('band', None, 'base'), may hold values from -6 to 6
- jones_deviation: float32 [16, 16, 8, 512], P('band', None, None, 'base'), may hold values from -1.8 to 1.8
- antenna_first: int32 [4096], P('base'), may hold values from 0 to 511, as said below
- antenna_second: int32 [4096], P('base'), may hold values from 0 to 511, as said below
Outputs:
- jones: float32 [16, 16, 8, 512], P('band', None, None, 'base')
- residual: float32 [16, 8, 4096], P('band', None, 'base')
Inputs may be any that keep to these rules, and one draw needn't show every extreme that they name: `antenna_first`: every station is the first station of exactly 8 baselines. On every baseline antenna_second differs from antenna_first.
All inputs are finite; a program needn't handle non-finite values.
Results may differ from a plain program's by a relative error of at most 0.0003.
Values sent between devices are 32-bit elements; how exact they have to be, the bound alone decides.
A program may use at most 128 MiB of HBM per device.

v0:
```python
import jax
import jax.numpy as jnp
from jax import lax
from jax.sharding import PartitionSpec as P

ITERS = 3
step_gain = 1.2
penalty_gain = 0.25


def expand_matrix(packed):
    return [
        [(packed[..., 0, :], packed[..., 1, :]), (packed[..., 2, :], packed[..., 3, :])],
        [(packed[..., 4, :], packed[..., 5, :]), (packed[..., 6, :], packed[..., 7, :])],
    ]


def pack_matrix(matrix):
    return jnp.stack(
        [
            matrix[0][0][0],
            matrix[0][0][1],
            matrix[0][1][0],
            matrix[0][1][1],
            matrix[1][0][0],
            matrix[1][0][1],
            matrix[1][1][0],
            matrix[1][1][1],
        ],
        axis=-2,
    )


def complex_mul(first_term, second_term):
    return (
        first_term[0] * second_term[0] - first_term[1] * second_term[1],
        first_term[0] * second_term[1] + first_term[1] * second_term[0],
    )


def complex_add(first_term, second_term):
    return (first_term[0] + second_term[0], first_term[1] + second_term[1])


def element_of(matrix, i, j, adjoint):
    if adjoint:
        return (matrix[j][i][0], -matrix[j][i][1])
    return matrix[i][j]


def matrix_product(first_factor, second_factor, adjoint_first=False, adjoint_second=False):
    result_rows = []
    for i in range(2):
        row_items = []
        for j in range(2):
            row_items.append(
                complex_add(
                    complex_mul(
                        element_of(first_factor, i, 0, adjoint_first),
                        element_of(second_factor, 0, j, adjoint_second),
                    ),
                    complex_mul(
                        element_of(first_factor, i, 1, adjoint_first),
                        element_of(second_factor, 1, j, adjoint_second),
                    ),
                )
            )
        result_rows.append(row_items)
    return result_rows


def fit_basis(band_count):
    positions = (2.0 * jnp.arange(band_count, dtype=jnp.float32) + 1.0) / band_count - 1.0
    columns = []
    for power in range(4):
        vector = positions**power
        for earlier in columns:
            vector = vector - jnp.sum(earlier * vector) * earlier
        vector = vector / jnp.sqrt(jnp.sum(vector * vector))
        columns.append(vector)
    return jnp.stack(columns, axis=1)


def local_gradients(
    leading_rows, trailing_rows, coherency, observed, antenna_first, antenna_second, station_number
):
    leading_jones = expand_matrix(leading_rows)
    trailing_jones = expand_matrix(trailing_rows)
    sky = expand_matrix(coherency)
    model = pack_matrix(
        matrix_product(leading_jones, matrix_product(sky, trailing_jones, adjoint_second=True))
    )
    residual = observed - jnp.sum(model, axis=1)
    resid_parts = expand_matrix(residual[:, None])
    gradient_leading = pack_matrix(
        matrix_product(resid_parts, matrix_product(trailing_jones, sky, adjoint_second=True))
    )
    gradient_trailing = pack_matrix(
        matrix_product(resid_parts, matrix_product(leading_jones, sky), adjoint_first=True)
    )
    shape_out = (coherency.shape[0], coherency.shape[1], 8, station_number)
    gradient_list = (
        jnp.zeros(shape_out, jnp.float32)
        .at[:, :, :, antenna_first]
        .add(gradient_leading)
        .at[:, :, :, antenna_second]
        .add(gradient_trailing)
    )
    return (gradient_list, residual)


def per_device(coherency, observed, jones_deviation, antenna_first, antenna_second):
    highest = lax.Precision.HIGHEST
    base_count = lax.axis_size("base")
    band_count = lax.axis_size("band")
    sub_dev = coherency.shape[0]
    base_dev = coherency.shape[-1]
    own_stations = jones_deviation.shape[-1]
    station_number = own_stations * base_count
    baseline_count = base_dev * base_count
    step_size = step_gain * station_number / baseline_count
    penalty = penalty_gain * baseline_count / station_number
    poly_basis = fit_basis(sub_dev * band_count)
    local_basis = lax.dynamic_slice_in_dim(poly_basis, lax.axis_index("band") * sub_dev, sub_dev, 0)
    identity = jnp.array([1.0, 0.0, 0.0, 0.0, 0.0, 0.0, 1.0, 0.0], dtype=jnp.float32)[:, None]
    jones_current = identity + jones_deviation
    jones_current = lax.all_gather(jones_current, "base", axis=3, tiled=True)
    consensus = jones_current
    dual_var = jnp.zeros_like(jones_current)
    residual = None
    for iteration in range(ITERS):
        leading_rows = jnp.take(jones_current, antenna_first, axis=3)
        trailing_rows = jnp.take(jones_current, antenna_second, axis=3)
        local_terms, residual = local_gradients(
            leading_rows,
            trailing_rows,
            coherency,
            observed,
            antenna_first,
            antenna_second,
            station_number,
        )
        station_gradients = lax.psum(local_terms, "base")
        jones_current = jones_current + step_size * (
            station_gradients - dual_var - penalty * (jones_current - consensus)
        )
        if iteration + 1 < ITERS:
            target = jones_current + dual_var / penalty
            partial_fit = jnp.einsum("fm,fkcs->mkcs", local_basis, target, precision=highest)
            coefficients = lax.psum(partial_fit, "band")
            consensus = jnp.einsum("fm,mkcs->fkcs", local_basis, coefficients, precision=highest)
            dual_var = dual_var + penalty * (jones_current - consensus)
    jones_current = lax.dynamic_slice_in_dim(
        jones_current, lax.axis_index("base") * own_stations, own_stations, 3
    )
    return (jones_current, residual)


def solution(mesh):
    return jax.shard_map(
        per_device,
        mesh=mesh,
        in_specs=(
            P("band", None, None, "base"),
            P("band", None, "base"),
            P("band", None, None, "base"),
            P("base"),
            P("base"),
        ),
        out_specs=(P("band", None, None, "base"), P("band", None, "base")),
        check_vma=False,
    )
```

profile of v0, /device:TPU:0, one launch (start us, length us, event | category | flops | bytes accessed | tf_op | source)
XLA Modules:
  0.0 1139.3 jit_solution(16276159739745969013)
XLA Ops:
  19.4 120.1 %all-gather.2.cloned.1.call-done = f32[8,16,8,512]{1,2,0,3:T(8,128)} async-done(((f32[8,16,8,32]{1,2,0,3:T(8,128)}), f32[8,16,8,512]{1,2,0,3:T(8,128)}) %all-gather.2.cloned.1.call-update) | async-done | bytes 2097168 | tf_op jit(solution)/shard_map/all_gather | solution.py:127
  139.5 11.4 copy.497
  150.9 10.6 gather_fusion
  168.6 10.6 gather_fusion.1
  254.8 39.8 %scatter_fusion = f32[8,16,8,512]{1,2,3,0:T(8,128)} fusion(f32[8,16,8,512]{1,2,3,0:T(8,128)} %broadcast.414.clone, s32[256]{0:T(256)S(1)} %copy-done.42, f32[256,8,16,8]{2,3,1,0:T(8,128)} %copy.527), kind=kCustom, calls=%fused_computation.6 | custom fusion | flops 262144 | bytes 3146752 | tf_op jit(solution)/shard_map/scatter-add | solution.py:105
  294.7 39.9 %scatter_fusion.1 = f32[8,16,8,512]{1,2,3,0:T(8,128)} fusion(f32[8,16,8,512]{1,2,3,0:T(8,128)} %scatter_fusion, s32[256]{0:T(256)S(1)} %copy-done.38, f32[256,8,16,8]{2,3,1,0:T(8,128)} %copy.536), kind=kCustom, calls=%fused_computation.7 | custom fusion | flops 262144 | bytes 3146752 | tf_op jit(solution)/shard_map/scatter-add | solution.py:107
  334.6 9.7 copy.537
  350.6 12.2 %copy.540 = f32[8,16,8,512]{3,0,2,1:T(8,128)} copy(f32[8,16,8,512]{1,2,0,3:T(8,128)} %all-gather.2.cloned.1.call-done) | data formatting | bytes 4194304 | tf_op jit(solution)/shard_map/all_gather | solution.py:127
  362.8 78.2 %all-reduce.6.cloned.1.call-done = f32[8,16,8,512]{3,0,2,1:T(8,128)} async-done(((f32[8,16,8,512]{3,0,2,1:T(8,128)}), f32[8,16,8,512]{3,0,2,1:T(8,128)}) %all-reduce.6.cloned.1.call-update) | async-done | bytes 2097168 | tf_op jit(solution)/shard_map/psum | solution.py:143
  443.8 7.8 copy.541
  451.6 10.8 gather_fusion.2
  462.4 10.8 gather_fusion.3
  586.2 39.8 %scatter_fusion.2 = f32[8,16,8,512]{1,2,3,0:T(8,128)} fusion(f32[8,16,8,512]{1,2,3,0:T(8,128)} %broadcast.414.clone.1, s32[256]{0:T(256)S(1)} %copy-done.43, f32[256,8,16,8]{2,3,1,0:T(8,128)} %copy.563), kind=kCustom, calls=%fused_computation.8 | custom fusion | flops 262144 | bytes 3146752 | tf_op jit(solution)/shard_map/scatter-add | solution.py:105
  626.0 39.8 %scatter_fusion.3 = f32[8,16,8,512]{1,2,3,0:T(8,128)} fusion(f32[8,16,8,512]{1,2,3,0:T(8,128)} %scatter_fusion.2, s32[256]{0:T(256)S(1)} %copy-done.39, f32[256,8,16,8]{2,3,1,0:T(8,128)} %copy.572), kind=kCustom, calls=%fused_computation.9 | custom fusion | flops 262144 | bytes 3146752 | tf_op jit(solution)/shard_map/scatter-add | solution.py:107
  665.8 9.7 copy.573
  686.7 86.7 %all-reduce.8.cloned.1.call-done = f32[8,16,8,512]{3,0,2,1:T(8,128)} async-done(((f32[8,16,8,512]{3,0,2,1:T(8,128)}), f32[8,16,8,512]{3,0,2,1:T(8,128)}) %all-reduce.8.cloned.1.call-update) | async-done | bytes 2097168 | tf_op jit(solution)/shard_map/psum | solution.py:143
  773.5 41.6 %all-reduce.10.cloned.1.call-done = f32[4,16,8,512]{3,0,2,1:T(4,128)} async-done(((f32[4,16,8,512]{3,0,2,1:T(4,128)}), f32[4,16,8,512]{3,0,2,1:T(4,128)}) %all-reduce.10.cloned.1.call-update) | async-done | bytes 1048592 | tf_op jit(solution)/shard_map/psum | solution.py:150
  828.8 10.8 gather_fusion.4
  839.6 10.8 gather_fusion.5
  912.8 8.4 copy.596
  940.7 39.8 %scatter_fusion.4 = f32[8,16,8,512]{1,2,3,0:T(8,128)} fusion(f32[8,16,8,512]{1,2,3,0:T(8,128)} %broadcast.414, s32[256]{0:T(256)S(1)} %copy-done.44, f32[256,8,16,8]{2,3,1,0:T(8,128)} %copy.596), kind=kCustom, calls=%fused_computation.10 | custom fusion | flops 262144 | bytes 3146752 | tf_op jit(solution)/shard_map/scatter-add | solution.py:105
  980.5 39.8 %scatter_fusion.5 = f32[8,16,8,512]{1,2,3,0:T(8,128)} fusion(f32[8,16,8,512]{1,2,3,0:T(8,128)} %scatter_fusion.4, s32[256]{0:T(256)S(1)} %copy-done.40, f32[256,8,16,8]{2,3,1,0:T(8,128)} %copy.605), kind=kCustom, calls=%fused_computation.11 | custom fusion | flops 262144 | bytes 3146752 | tf_op jit(solution)/shard_map/scatter-add | solution.py:107
  1020.3 10.1 copy.606
  1036.3 92.8 %all-reduce.12.cloned.1.call-done = f32[8,16,8,512]{3,0,2,1:T(8,128)} async-done(((f32[8,16,8,512]{3,0,2,1:T(8,128)}), f32[8,16,8,512]{3,0,2,1:T(8,128)}) %all-reduce.12.cloned.1.call-update) | async-done | bytes 2097168 | tf_op jit(solution)/shard_map/psum | solution.py:143
  (313 shorter events, 327.9 us)
Async XLA Ops:
  7.2 132.3 %all-gather.2.cloned.1.call-start = ((), (), s32[]{:S(2)}) async-start(), calls=%async_computation | async-start | bytes 17825792 | tf_op jit(solution)/shard_map/all_gather | solution.py:127
  10.2 430.8 %all-reduce.6.cloned.1.call-start = ((), (), s32[]{:S(2)}) async-start(), calls=%async_computation.1 | async-start | bytes 4194304 | tf_op jit(solution)/shard_map/psum | solution.py:143
  11.5 187.3 %copy-start.13 = (f32[8,8,256]{1,0,2:T(8,128)}, f32[8,8,256]{1,0,2:T(8,128)S(1)}, u32[]{:S(2)}) copy-start(f32[8,8,256]{1,0,2:T(8,128)S(1)} %copy.510) | copy-start | bytes 196612
  12.3 138.6 %copy-start.45 = (s32[1024]{0:T(1024)}, s32[1024]{0:T(1024)S(1)}, u32[]{:S(2)}) copy-start(s32[1024]{0:T(1024)S(1)} %pad_clamp_fusion.1) | copy-start | bytes 12292
  12.9 155.8 %copy-start.46 = (s32[1024]{0:T(1024)}, s32[1024]{0:T(1024)S(1)}, u32[]{:S(2)}) copy-start(s32[1024]{0:T(1024)S(1)} %pad_clamp_fusion) | copy-start | bytes 12292
  13.6 173.3 %copy-start.50 = (pred[256]{0:T(512)(128)(4,1)}, pred[256]{0:T(512)(128)(4,1)S(1)}, u32[]{:S(2)}) copy-start(pred[256]{0:T(512)(128)(4,1)S(1)} %get-tuple-element.206) | copy-start | bytes 772
  13.6 174.7 %copy-start.47 = (pred[256]{0:T(512)(128)(4,1)}, pred[256]{0:T(512)(128)(4,1)S(1)}, u32[]{:S(2)}) copy-start(pred[256]{0:T(512)(128)(4,1)S(1)} %get-tuple-element.205) | copy-start | bytes 772
  19.3 198.3 %copy-start.5 = (f32[8,16,1,256]{3,2,1,0:T(1,128)}, f32[8,16,1,256]{3,2,1,0:T(1,128)S(1)}, u32[]{:S(2)}) copy-start(f32[8,16,1,256]{3,2,1,0:T(1,128)S(1)} %get-tuple-element.140) | copy-start | bytes 393220
  19.3 198.3 %copy-start.7 = (f32[8,16,1,256]{3,2,1,0:T(1,128)}, f32[8,16,1,256]{3,2,1,0:T(1,128)S(1)}, u32[]{:S(2)}) copy-start(f32[8,16,1,256]{3,2,1,0:T(1,128)S(1)} %get-tuple-element.142) | copy-start | bytes 393220
  19.4 198.3 %copy-start.9 = (f32[8,16,1,256]{3,2,1,0:T(1,128)}, f32[8,16,1,256]{3,2,1,0:T(1,128)S(1)}, u32[]{:S(2)}) copy-start(f32[8,16,1,256]{3,2,1,0:T(1,128)S(1)} %get-tuple-element.145) | copy-start | bytes 393220
  19.4 198.3 %copy-start.11 = (f32[8,16,1,256]{3,2,1,0:T(1,128)}, f32[8,16,1,256]{3,2,1,0:T(1,128)S(1)}, u32[]{:S(2)}) copy-start(f32[8,16,1,256]{3,2,1,0:T(1,128)S(1)} %get-tuple-element.146) | copy-start | bytes 393220
  19.4 199.8 %copy-start.3 = (f32[8,16,1,256]{3,2,1,0:T(1,128)}, f32[8,16,1,256]{3,2,1,0:T(1,128)S(1)}, u32[]{:S(2)}) copy-start(f32[8,16,1,256]{3,2,1,0:T(1,128)S(1)} %get-tuple-element.147) | copy-start | bytes 393220
  247.8 46.9 %copy-start.38 = (s32[256]{0:T(256)S(1)}, s32[256]{0:T(256)}, u32[]{:S(2)}) copy-start(s32[256]{0:T(256)} %copy-done.37) | copy-start | bytes 3076
  344.3 429.2 %all-reduce.8.cloned.1.call-start = ((), (), s32[]{:S(2)}) async-start(), calls=%async_computation.2 | async-start | bytes 4194304 | tf_op jit(solution)/shard_map/psum | solution.py:143
  443.8 240.0 %copy-start.2 = (f32[8,16,8,512]{3,0,2,1:T(8,128)}, f32[8,16,8,512]{3,0,2,1:T(8,128)S(1)}, u32[]{:S(2)}) copy-start(f32[8,16,8,512]{3,0,2,1:T(8,128)S(1)} %multiply_add_fusion) | copy-start | bytes 6291460
  451.6 28.7 %copy-start.51 = (pred[256]{0:T(512)(128)(4,1)S(1)}, pred[256]{0:T(512)(128)(4,1)}, u32[]{:S(2)}) copy-start(pred[256]{0:T(512)(128)(4,1)} %copy-done.50) | copy-start | bytes 772
  473.2 16.0 %copy-start.48 = (pred[256]{0:T(512)(128)(4,1)S(1)}, pred[256]{0:T(512)(128)(4,1)}, u32[]{:S(2)}) copy-start(pred[256]{0:T(512)(128)(4,1)} %copy-done.47) | copy-start | bytes 772
  579.1 46.9 %copy-start.39 = (s32[256]{0:T(256)S(1)}, s32[256]{0:T(256)}, u32[]{:S(2)}) copy-start(s32[256]{0:T(256)} %copy-done.37) | copy-start | bytes 3076
  675.5 139.5 %all-reduce.10.cloned.1.call-start = ((), (), s32[]{:S(2)}) async-start(), calls=%async_computation.3 | async-start | bytes 2097152 | tf_op jit(solution)/shard_map/psum | solution.py:150
  683.8 145.0 %copy-start.35 = (f32[16,4]{0,1:T(4,128)}, f32[16,4]{0,1:T(4,128)S(1)}, u32[]{:S(2)}) copy-start(f32[16,4]{0,1:T(4,128)S(1)} %pad_maximum_fusion) | copy-start | bytes 772
  686.7 344.7 %all-reduce.14.cloned.1.call-start = ((), (), s32[]{:S(2)}) async-start(), calls=%async_computation.5 | async-start | bytes 2097152 | tf_op jit(solution)/shard_map/psum | solution.py:150
  828.8 27.8 %copy-start.52 = (pred[256]{0:T(512)(128)(4,1)S(1)}, pred[256]{0:T(512)(128)(4,1)}, u32[]{:S(2)}) copy-start(pred[256]{0:T(512)(128)(4,1)} %copy-done.50) | copy-start | bytes 772
  900.9 228.2 %all-reduce.12.cloned.1.call-start = ((), (), s32[]{:S(2)}) async-start(), calls=%async_computation.4 | async-start | bytes 4194304 | tf_op jit(solution)/shard_map/psum | solution.py:143
  933.6 46.9 %copy-start.40 = (s32[256]{0:T(256)S(1)}, s32[256]{0:T(256)}, u32[]{:S(2)}) copy-start(s32[256]{0:T(256)} %copy-done.37) | copy-start | bytes 3076
  (36 other events, 244.2 us)
Sparse Core Ops, SparseCore 0:
  10.3 129.1 all-gather.1
  344.4 96.5 all-reduce.5
  675.6 97.8 all-reduce.7
  775.6 39.3 all-reduce.9
  901.0 40.0 all-reduce.13
  1030.6 98.4 all-reduce.11
where the time goes:
time: 1150 us; the launch traced here: 1140 us
  waiting for transfers between devices  419 us (36%)
  local copies, waits for them, and re-layouts  357 us (31%)
  other arithmetic  324 us (28%)
  between operations  19.6 us (2%)
  matrix products  18.7 us (2%)
    psum x3, waiting for transfers between devices, per_device(): station_gradients = lax.psum(local_terms, 'base')  258 us
    scatter-add x6, other arithmetic, local_gradients(): gradient_list = jnp.zeros(shape_out, jnp.float32).at[:, :, :, antenna_fir...  239 us
    all_gather x1, waiting for transfers between devices, per_device(): jones_current = lax.all_gather(jones_current, 'base', axis=3, tiled=True)  120 us
    another operation x12, local copies, waits for them, and re-layouts, pack_matrix(): jnp.stack([matrix[0][0][0], matrix[0][0][1], matrix[0][1][0], matrix[0][1...  61.1 us
    gather x6, local copies, waits for them, and re-layouts, per_device(): trailing_rows = jnp.take(jones_current, antenna_second, axis=3)  53.9 us
    gather x6, local copies, waits for them, and re-layouts, per_device(): leading_rows = jnp.take(jones_current, antenna_first, axis=3)  52.7 us
    psum x2, waiting for transfers between devices, per_device(): coefficients = lax.psum(partial_fit, 'band')  41.6 us
    scatter-add x3, local copies, waits for them, and re-layouts, local_gradients(): gradient_list = jnp.zeros(shape_out, jnp.float32).at[:, :, :, antenna_fir...  29.5 us
  transfers between devices with their start and end apart: 6, of which 5 were waited for; matrix products, arithmetic and copies ran while one was open for 15% of the time, Pallas kernels for 0%

commit v1 on v0

--- a/solution.py
+++ b/solution.py
@@ -1,3 +1,4 @@
+import functools
 import jax
 import jax.numpy as jnp
 from jax import lax
@@ -6,6 +7,14 @@
 ITERS = 3
 step_gain = 1.2
 penalty_gain = 0.25
+
+
+def remake_spot_now(local, device_axis):
+    w_next = jnp.sum(jax.lax.all_gather(local, device_axis), 0)
+    return w_next
+
+
+follow_outputs = functools.partial(remake_spot_now, device_axis="base")
 
 
 def expand_matrix(packed):
@@ -140,7 +149,7 @@
             antenna_second,
             station_number,
         )
-        station_gradients = lax.psum(local_terms, "base")
+        station_gradients = follow_outputs(local_terms)
         jones_current = jones_current + step_size * (
             station_gradients - dual_var - penalty * (jones_current - consensus)
         )

time: 1150 us -> 1400 us (1.22)
  waiting for transfers between devices: 419 us -> 614 us
  other arithmetic: 324 us -> 372 us
    all_gather x0 -> x3, waiting for transfers between devices: none -> 466 us  [remake_spot_now(): w_next = jnp.sum(jax.lax.all_gather(local, device_axis), 0)]
    psum x3 -> x0, waiting for transfers between devices: 258 us -> none  [per_device(): station_gradients = lax.psum(local_terms, 'base')]
    reduce_sum x0 -> x3, other arithmetic: none -> 42.8 us  [remake_spot_now(): w_next = jnp.sum(jax.lax.all_gather(local, device_axis), 0)]
  transfers between devices with their start and end apart: 6 -> 6, of which waited for: 5 -> 5; matrix products, arithmetic and copies ran while one was open for 15% -> 14% of each run, Pallas kernels for 0% -> 0%
where the time goes in v1:
time: 1400 us; the launch traced here: 1390 us
  waiting for transfers between devices  614 us (44%)
  other arithmetic  372 us (27%)
  local copies, waits for them, and re-layouts  361 us (26%)
  matrix products  20.1 us (1%)
  between operations  19.4 us (1%)
    all_gather x3, waiting for transfers between devices, remake_spot_now(): w_next = jnp.sum(jax.lax.all_gather(local, device_axis), 0)  466 us
    scatter-add x6, other arithmetic, local_gradients(): gradient_list = jnp.zeros(shape_out, jnp.float32).at[:, :, :, antenna_fir...  239 us
    all_gather x1, waiting for transfers between devices, per_device(): jones_current = lax.all_gather(jones_current, 'base', axis=3, tiled=True)  120 us
    another operation x12, local copies, waits for them, and re-layouts, pack_matrix(): jnp.stack([matrix[0][0][0], matrix[0][0][1], matrix[0][1][0], matrix[0][1...  61.5 us
    gather x6, local copies, waits for them, and re-layouts, per_device(): leading_rows = jnp.take(jones_current, antenna_first, axis=3)  54.5 us
    gather x6, local copies, waits for them, and re-layouts, per_device(): trailing_rows = jnp.take(jones_current, antenna_second, axis=3)  52.1 us
    reduce_sum x3, other arithmetic, remake_spot_now(): w_next = jnp.sum(jax.lax.all_gather(local, device_axis), 0)  42.8 us
    scatter-add x3, local copies, waits for them, and re-layouts, local_gradients(): gradient_list = jnp.zeros(shape_out, jnp.float32).at[:, :, :, antenna_fir...  33.6 us
  transfers between devices with their start and end apart: 6, of which 5 were waited for; matrix products, arithmetic and copies ran while one was open for 14% of the time, Pallas kernels for 0%

profile of v1, /device:TPU:0, one launch (start us, length us, event | category | flops | bytes accessed | tf_op | source)
XLA Modules:
  0.0 1387.2 jit_solution(1346328054872452884)
XLA Ops:
  19.3 120.2 %all-gather.8.cloned.1.call-done = f32[8,16,8,512]{1,2,0,3:T(8,128)} async-done(((f32[8,16,8,32]{1,2,0,3:T(8,128)}), f32[8,16,8,512]{1,2,0,3:T(8,128)}) %all-gather.8.cloned.1.call-update) | async-done | bytes 2097168 | tf_op jit(solution)/shard_map/all_gather | solution.py:136
  139.5 11.4 copy.509
  150.9 10.7 gather_fusion
  255.2 39.8 %scatter_fusion = f32[8,16,8,512]{1,2,3,0:T(8,128)} fusion(f32[8,16,8,512]{1,2,3,0:T(8,128)} %broadcast.414.clone, s32[256]{0:T(256)S(1)} %copy-done.53, f32[256,8,16,8]{2,3,1,0:T(8,128)} %copy.539), kind=kCustom, calls=%fused_computation.6 | custom fusion | flops 262144 | bytes 3146752 | tf_op jit(solution)/shard_map/scatter-add | solution.py:114
  295.0 39.9 %scatter_fusion.1 = f32[8,16,8,512]{1,2,3,0:T(8,128)} fusion(f32[8,16,8,512]{1,2,3,0:T(8,128)} %scatter_fusion, s32[256]{0:T(256)S(1)} %copy-done.49, f32[256,8,16,8]{2,3,1,0:T(8,128)} %copy.548), kind=kCustom, calls=%fused_computation.7 | custom fusion | flops 262144 | bytes 3146752 | tf_op jit(solution)/shard_map/scatter-add | solution.py:116
  334.9 11.1 copy.549
  346.1 12.9 copy.554
  359.0 153.5 %all-gather.10.cloned.1.call-done = f32[128,16,8,512]{3,2,1,0:T(8,128)} async-done(((f32[8,16,8,512]{3,2,1,0:T(8,128)}), f32[128,16,8,512]{3,2,1,0:T(8,128)}) %all-gather.10.cloned.1.call-update) | async-done | bytes 33554448 | tf_op jit(solution)/shard_map/all_gather | solution.py:13
  512.5 14.1 %reduce_sum.140 = f32[8,16,8,512]{3,2,1,0:T(8,128)} reduce(f32[16,8,16,8,512]{4,3,2,1,0:T(8,128)} %bitcast.82, f32[]{:T(128)} %constant.23.clone.1), dimensions={0}, to_apply=%region_3.5 | reduce | flops 7864320 | bytes 35651588 | tf_op jit(solution)/shard_map/reduce_sum | solution.py:13
  538.6 10.8 gather_fusion.3
  549.4 10.8 gather_fusion.2
  670.7 39.8 %scatter_fusion.2 = f32[8,16,8,512]{1,2,3,0:T(8,128)} fusion(f32[8,16,8,512]{1,2,3,0:T(8,128)} %broadcast.414.clone.1, s32[256]{0:T(256)S(1)} %copy-done.54, f32[256,8,16,8]{2,3,1,0:T(8,128)} %copy.577), kind=kCustom, calls=%fused_computation.8 | custom fusion | flops 262144 | bytes 3146752 | tf_op jit(solution)/shard_map/scatter-add | solution.py:114
  710.5 39.9 %scatter_fusion.3 = f32[8,16,8,512]{1,2,3,0:T(8,128)} fusion(f32[8,16,8,512]{1,2,3,0:T(8,128)} %scatter_fusion.2, s32[256]{0:T(256)S(1)} %copy-done.50, f32[256,8,16,8]{2,3,1,0:T(8,128)} %copy.586), kind=kCustom, calls=%fused_computation.9 | custom fusion | flops 262144 | bytes 3146752 | tf_op jit(solution)/shard_map/scatter-add | solution.py:116
  750.4 11.1 copy.587
  779.0 150.7 %all-gather.12.cloned.1.call-done = f32[128,16,8,512]{3,2,1,0:T(8,128)} async-done(((f32[8,16,8,512]{3,2,1,0:T(8,128)}), f32[128,16,8,512]{3,2,1,0:T(8,128)}) %all-gather.12.cloned.1.call-update) | async-done | bytes 33554448 | tf_op jit(solution)/shard_map/all_gather | solution.py:13
  929.7 14.7 %reduce_sum.142 = f32[8,16,8,512]{3,2,1,0:T(8,128)} reduce(f32[16,8,16,8,512]{4,3,2,1,0:T(8,128)} %bitcast.80, f32[]{:T(128)} %constant.23.clone.1), dimensions={0}, to_apply=%region_7.9 | reduce | flops 7864320 | bytes 35651588 | tf_op jit(solution)/shard_map/reduce_sum | solution.py:13
  944.4 27.6 %all-reduce.3.cloned.1.call-done = f32[4,16,8,512]{3,0,2,1:T(4,128)} async-done(((f32[4,16,8,512]{3,0,2,1:T(4,128)}), f32[4,16,8,512]{3,0,2,1:T(4,128)}) %all-reduce.3.cloned.1.call-update) | async-done | bytes 1048592 | tf_op jit(solution)/shard_map/psum | solution.py:159
  986.9 10.8 gather_fusion.5
  997.7 10.8 gather_fusion.4
  1103.1 39.8 %scatter_fusion.4 = f32[8,16,8,512]{1,2,3,0:T(8,128)} fusion(f32[8,16,8,512]{1,2,3,0:T(8,128)} %broadcast.414, s32[256]{0:T(256)S(1)} %copy-done.55, f32[256,8,16,8]{2,3,1,0:T(8,128)} %copy.612), kind=kCustom, calls=%fused_computation.10 | custom fusion | flops 262144 | bytes 3146752 | tf_op jit(solution)/shard_map/scatter-add | solution.py:114
  1142.8 39.9 %scatter_fusion.5 = f32[8,16,8,512]{1,2,3,0:T(8,128)} fusion(f32[8,16,8,512]{1,2,3,0:T(8,128)} %scatter_fusion.4, s32[256]{0:T(256)S(1)} %copy-done.51, f32[256,8,16,8]{2,3,1,0:T(8,128)} %copy.621), kind=kCustom, calls=%fused_computation.11 | custom fusion | flops 262144 | bytes 3146752 | tf_op jit(solution)/shard_map/scatter-add | solution.py:116
  1182.8 11.3 copy.622
  1199.9 162.3 %all-gather.14.cloned.1.call-done = f32[128,16,8,512]{3,2,1,0:T(8,128)} async-done(((f32[8,16,8,512]{3,2,1,0:T(8,128)}), f32[128,16,8,512]{3,2,1,0:T(8,128)}) %all-gather.14.cloned.1.call-update) | async-done | bytes 33554448 | tf_op jit(solution)/shard_map/all_gather | solution.py:13
  1362.2 14.1 %reduce_sum.153 = f32[8,16,8,512]{3,2,1,0:T(8,128)} reduce(f32[16,8,16,8,512]{4,3,2,1,0:T(8,128)} %bitcast.81, f32[]{:T(128)} %constant.23.clone.1), dimensions={0}, to_apply=%region_21.23 | reduce | flops 7864320 | bytes 35651588 | tf_op jit(solution)/shard_map/reduce_sum | solution.py:13
  (337 shorter events, 359.8 us)
Async XLA Ops:
  7.2 132.3 %all-gather.8.cloned.1.call-start = ((), (), s32[]{:S(2)}) async-start(), calls=%async_computation | async-start | bytes 17825792 | tf_op jit(solution)/shard_map/all_gather | solution.py:136
  10.2 502.3 %all-gather.10.cloned.1.call-start = ((), (), s32[]{:S(2)}) async-start(), calls=%async_computation.3 | async-start | bytes 35651584 | tf_op jit(solution)/shard_map/all_gather | solution.py:13
  11.5 187.1 %copy-start.13 = (f32[8,8,256]{1,0,2:T(8,128)}, f32[8,8,256]{1,0,2:T(8,128)S(1)}, u32[]{:S(2)}) copy-start(f32[8,8,256]{1,0,2:T(8,128)S(1)} %copy.522) | copy-start | bytes 196612
  12.3 138.6 %copy-start.56 = (s32[1024]{0:T(1024)}, s32[1024]{0:T(1024)S(1)}, u32[]{:S(2)}) copy-start(s32[1024]{0:T(1024)S(1)} %pad_clamp_fusion.1) | copy-start | bytes 12292
  12.9 155.8 %copy-start.57 = (s32[1024]{0:T(1024)}, s32[1024]{0:T(1024)S(1)}, u32[]{:S(2)}) copy-start(s32[1024]{0:T(1024)S(1)} %pad_clamp_fusion) | copy-start | bytes 12292
  13.6 173.1 %copy-start.58 = (pred[256]{0:T(512)(128)(4,1)}, pred[256]{0:T(512)(128)(4,1)S(1)}, u32[]{:S(2)}) copy-start(pred[256]{0:T(512)(128)(4,1)S(1)} %get-tuple-element.206) | copy-start | bytes 772
  13.6 174.5 %copy-start.61 = (pred[256]{0:T(512)(128)(4,1)}, pred[256]{0:T(512)(128)(4,1)S(1)}, u32[]{:S(2)}) copy-start(pred[256]{0:T(512)(128)(4,1)S(1)} %get-tuple-element.205) | copy-start | bytes 772
  19.3 198.3 %copy-start.5 = (f32[8,16,1,256]{3,2,1,0:T(1,128)}, f32[8,16,1,256]{3,2,1,0:T(1,128)S(1)}, u32[]{:S(2)}) copy-start(f32[8,16,1,256]{3,2,1,0:T(1,128)S(1)} %get-tuple-element.140) | copy-start | bytes 393220
  19.3 198.3 %copy-start.7 = (f32[8,16,1,256]{3,2,1,0:T(1,128)}, f32[8,16,1,256]{3,2,1,0:T(1,128)S(1)}, u32[]{:S(2)}) copy-start(f32[8,16,1,256]{3,2,1,0:T(1,128)S(1)} %get-tuple-element.141) | copy-start | bytes 393220
  19.3 198.3 %copy-start.9 = (f32[8,16,1,256]{3,2,1,0:T(1,128)}, f32[8,16,1,256]{3,2,1,0:T(1,128)S(1)}, u32[]{:S(2)}) copy-start(f32[8,16,1,256]{3,2,1,0:T(1,128)S(1)} %get-tuple-element.142) | copy-start | bytes 393220
  19.3 198.3 %copy-start.11 = (f32[8,16,1,256]{3,2,1,0:T(1,128)}, f32[8,16,1,256]{3,2,1,0:T(1,128)S(1)}, u32[]{:S(2)}) copy-start(f32[8,16,1,256]{3,2,1,0:T(1,128)S(1)} %get-tuple-element.147) | copy-start | bytes 393220
  19.3 199.9 %copy-start.3 = (f32[8,16,1,256]{3,2,1,0:T(1,128)}, f32[8,16,1,256]{3,2,1,0:T(1,128)S(1)}, u32[]{:S(2)}) copy-start(f32[8,16,1,256]{3,2,1,0:T(1,128)S(1)} %get-tuple-element.146) | copy-start | bytes 393220
  248.1 46.9 %copy-start.49 = (s32[256]{0:T(256)S(1)}, s32[256]{0:T(256)}, u32[]{:S(2)}) copy-start(s32[256]{0:T(256)} %copy-done.48) | copy-start | bytes 3076
  346.0 583.7 %all-gather.12.cloned.1.call-start = ((), (), s32[]{:S(2)}) async-start(), calls=%async_computation.4 | async-start | bytes 35651584 | tf_op jit(solution)/shard_map/all_gather | solution.py:13
  530.9 245.2 %copy-start.2 = (f32[8,16,8,512]{3,0,2,1:T(8,128)}, f32[8,16,8,512]{3,0,2,1:T(8,128)S(1)}, u32[]{:S(2)}) copy-start(f32[8,16,8,512]{3,0,2,1:T(8,128)S(1)} %fusion.3) | copy-start | bytes 6291460
  538.6 27.9 %copy-start.62 = (pred[256]{0:T(512)(128)(4,1)S(1)}, pred[256]{0:T(512)(128)(4,1)}, u32[]{:S(2)}) copy-start(pred[256]{0:T(512)(128)(4,1)} %copy-done.61) | copy-start | bytes 772
  663.6 46.9 %copy-start.50 = (s32[256]{0:T(256)S(1)}, s32[256]{0:T(256)}, u32[]{:S(2)}) copy-start(s32[256]{0:T(256)} %copy-done.48) | copy-start | bytes 3076
  761.6 210.4 %all-reduce.3.cloned.1.call-start = ((), (), s32[]{:S(2)}) async-start(), calls=%async_computation.1 | async-start | bytes 2097152 | tf_op jit(solution)/shard_map/psum | solution.py:159
  776.1 195.9 %copy-start.46 = (f32[16,4]{0,1:T(4,128)}, f32[16,4]{0,1:T(4,128)S(1)}, u32[]{:S(2)}) copy-start(f32[16,4]{0,1:T(4,128)S(1)} %pad_maximum_fusion) | copy-start | bytes 772
  779.0 416.1 %all-reduce.5.cloned.1.call-start = ((), (), s32[]{:S(2)}) async-start(), calls=%async_computation.2 | async-start | bytes 2097152 | tf_op jit(solution)/shard_map/psum | solution.py:159
  986.9 27.9 %copy-start.63 = (pred[256]{0:T(512)(128)(4,1)S(1)}, pred[256]{0:T(512)(128)(4,1)}, u32[]{:S(2)}) copy-start(pred[256]{0:T(512)(128)(4,1)} %copy-done.61) | copy-start | bytes 772
  1054.3 308.0 %all-gather.14.cloned.1.call-start = ((), (), s32[]{:S(2)}) async-start(), calls=%async_computation.5 | async-start | bytes 35651584 | tf_op jit(solution)/shard_map/all_gather | solution.py:13
  1062.2 21.3 %copy-start.15 = (f32[8,16,8,256]{3,1,2,0:T(8,128)S(1)}, f32[8,16,8,256]{3,1,2,0:T(8,128)}, u32[]{:S(2)}) copy-start(f32[8,16,8,256]{3,1,2,0:T(8,128)} %copy-done.14) | copy-start | bytes 3145732
  1095.9 46.9 %copy-start.51 = (s32[256]{0:T(256)S(1)}, s32[256]{0:T(256)}, u32[]{:S(2)}) copy-start(s32[256]{0:T(256)} %copy-done.48) | copy-start | bytes 3076
  (46 other events, 389.8 us)
Sparse Core Ops, SparseCore 0:
  10.3 129.1 all-gather.7
  346.2 166.3 all-gather.9
  761.7 167.9 all-gather.11
  931.9 40.0 all-reduce.2
  1054.4 40.0 all-reduce.4
  1194.2 167.9 all-gather.13
